TPU v7x, 32 devices: a whole 2x2x4 slice. The times are simulated.
32 devices in a mesh: fsdp: 4 (over y, core), ctx: 2 (over x), tp: 4 (over z).
Axes of the slice: x: 2, y: 2, z: 4, core: 2. Of those that a mesh axis runs over, the one named last changes fastest.
Arguments:
- inputs: bfloat16 [2, 8, 512, 1024], P(None, 'fsdp', 'ctx'), may hold values from -6 to 6
- out_grad: bfloat16 [2, 8, 512, 1024], P(None, 'fsdp', 'ctx'), may hold values from -6 to 6
- segment_ids: int32 [2, 8, 512], P(None, 'fsdp'), may hold values from 0 to 7, never falling along the last dimension, each value on 1 to 256 neighbouring positions
- w_qkv: bfloat16 [1024, 3072], P(('fsdp', 'ctx'), 'tp'), may hold values from -0.25 to 0.25
- bias_qv: bfloat16 [2048], P('tp'), may hold values from -3 to 3
- w_out: bfloat16 [1024, 1024], P(('fsdp', 'ctx'), 'tp'), may hold values from -0.25 to 0.25
- w_up: bfloat16 [1024, 4096], P(('fsdp', 'ctx'), 'tp'), may hold values from -0.1875 to 0.1875
- bias_up: bfloat16 [4096], P('tp'), may hold values from -2 to 2
- w_down: bfloat16 [1024, 4096], P(('fsdp', 'ctx'), 'tp'), may hold values from -0.125 to 0.125
- gains: bfloat16 [1024, 2], P(('fsdp', 'ctx')), may hold values from 0.25 to 1.75
- shifts: bfloat16 [1024, 4], P(('fsdp', 'ctx')), may hold values from -2 to 2
Outputs:
- layer_out: bfloat16 [2, 8, 512, 1024], P(None, 'fsdp', ('ctx', 'tp'))
- input_grad: float32 [2, 8, 512, 1024], P(None, 'fsdp', ('ctx', 'tp'))
- grad_w_qkv: float32 [1024, 3072], P(('fsdp', 'ctx'), 'tp')
- grad_bias_qv: float32 [2048], P('tp')
- grad_w_out: float32 [1024, 1024], P(('fsdp', 'ctx'), 'tp')
- grad_w_up: float32 [1024, 4096], P(('fsdp', 'ctx'), 'tp')
- grad_bias_up: float32 [4096], P('tp')
- grad_w_down: float32 [1024, 4096], P(('fsdp', 'ctx'), 'tp')
- grad_gains: float32 [1024, 2], P(('fsdp', 'ctx'))
- grad_shifts: float32 [1024, 4], P(('fsdp', 'ctx'))
Inputs may be any that keep to these rules, and one draw needn't show every extreme that they name: `segment_ids`: within a sequence the ids never fall; each of the 8 documents holds 1 to 256 positions, and one holds exactly 256.
All inputs are finite; a program needn't handle non-finite values.
Results may differ from a plain program's by a relative error of at most 0.018.
Values may be sent and summed in bfloat16 or wider, within the bound.
A program may use at most 64 MiB of HBM per device.

v0:
```python
import jax
import jax.numpy as jnp
from jax import lax
from jax.experimental import pallas as pl
from jax.experimental.pallas import tpu as pltpu
from jax.sharding import PartitionSpec as P

HD = 64


norm_epsilon = 1e-12
masked_score = -1e30


def norm_rows(rows_in, gain_row, offset):
    average = jnp.mean(rows_in, axis=-1, keepdims=True)
    centered = rows_in - average
    spread = jnp.mean(centered * centered, axis=-1, keepdims=True)
    return centered * lax.rsqrt(spread + norm_epsilon) * gain_row + offset


def exact_gelu(rows_in):
    return jax.nn.gelu(rows_in, approximate=False)


def contract_rows(left_rows, right_rows):
    return lax.dot_general(
        left_rows, right_rows, (((0,), (0,)), ((), ())), preferred_element_type=jnp.float32
    )


def times_transposed(left_rows, right_rows):
    return lax.dot_general(
        left_rows, right_rows, (((1,), (1,)), ((), ())), preferred_element_type=jnp.float32
    )


def masked_scores(queries, key_rows, same_segment, score_scale):
    scores = (
        jnp.einsum("sqhe,skhe->shqk", queries, key_rows, preferred_element_type=jnp.float32)
        * score_scale
    )
    return jnp.where(same_segment[:, None], scores, masked_score)


def add_pair(running, update):
    return running + update


def reduce_rows(part):
    return lax.psum(part, "tp")


def local(
    inputs, out_grad, segment_ids, w_qkv, bias_qv, w_out, w_up, bias_up, w_down, gains, shifts
):
    batches, seq_local, rows_local, model_width = inputs.shape
    tokens = seq_local * rows_local
    heads_local = w_out.shape[1] // HD
    score_scale = HD ** (-0.5)
    row_share = rows_local // lax.axis_size("tp")
    row_start = lax.axis_index("tp") * row_share
    query_start = lax.axis_index("ctx") * rows_local
    qv_bias = bias_qv.astype(jnp.float32).reshape(heads_local, 2, HD)
    up_bias = bias_up.astype(jnp.float32)

    def pick_rows(values):
        shaped = values.reshape(seq_local, rows_local, model_width)
        return lax.dynamic_slice_in_dim(shaped, row_start, row_share, 1)

    full_totals = (
        jnp.zeros((model_width, w_qkv.shape[1]), jnp.float32),
        jnp.zeros((model_width, w_out.shape[1]), jnp.float32),
        jnp.zeros((model_width, w_up.shape[1]), jnp.float32),
        jnp.zeros((model_width, w_down.shape[1]), jnp.float32),
        jnp.zeros((model_width, 2), jnp.float32),
        jnp.zeros((model_width, 4), jnp.float32),
    )
    share_totals = (
        jnp.zeros(w_qkv.shape, jnp.float32),
        jnp.zeros(w_out.shape, jnp.float32),
        jnp.zeros(w_up.shape, jnp.float32),
        jnp.zeros(w_down.shape, jnp.float32),
        jnp.zeros(gains.shape, jnp.float32),
        jnp.zeros(shifts.shape, jnp.float32),
    )
    qv_bias_grad = jnp.zeros(bias_qv.shape, jnp.float32)
    up_bias_grad = jnp.zeros(bias_up.shape, jnp.float32)
    layer_rows = []
    input_rows = []
    for batch_index in range(batches):
        gathered = (
            lax.all_gather(w_qkv, ("fsdp", "ctx"), axis=0, tiled=True),
            lax.all_gather(w_out, ("fsdp", "ctx"), axis=0, tiled=True),
            lax.all_gather(w_up, ("fsdp", "ctx"), axis=0, tiled=True),
            lax.all_gather(w_down, ("fsdp", "ctx"), axis=0, tiled=True),
            lax.all_gather(gains, ("fsdp", "ctx"), axis=0, tiled=True),
            lax.all_gather(shifts, ("fsdp", "ctx"), axis=0, tiled=True),
        )
        full_qkv, full_out, full_up, full_down, full_gains, full_shifts = gathered
        gain_rows = full_gains.astype(jnp.float32)
        shift_rows = full_shifts.astype(jnp.float32)
        x_low = inputs[batch_index].reshape(tokens, model_width)
        x_full = x_low.astype(jnp.float32)
        projected = jnp.dot(x_low, full_qkv, preferred_element_type=jnp.float32)
        projected = projected.reshape(seq_local, rows_local, heads_local, 3, HD)
        queries = (projected[:, :, :, 0] + qv_bias[:, 0]).astype(jnp.bfloat16)
        key_local = projected[:, :, :, 1].astype(jnp.bfloat16)
        value_local = (projected[:, :, :, 2] + qv_bias[:, 1]).astype(jnp.bfloat16)
        joined = jnp.concatenate([key_local, value_local], axis=-1)
        joined_all = lax.all_gather(joined, "ctx", axis=1, tiled=True)
        key_rows = joined_all[..., :HD]
        value_rows = joined_all[..., HD:]
        segments = segment_ids[batch_index]
        query_segments = lax.dynamic_slice_in_dim(segments, query_start, rows_local, 1)
        same_segment = query_segments[:, :, None] == segments[:, None, :]
        scores = masked_scores(queries, key_rows, same_segment, score_scale)
        row_max = jnp.max(scores, axis=-1, keepdims=True)
        weights = jnp.exp(scores - row_max)
        row_total = jnp.sum(weights, axis=-1, keepdims=True)
        log_total = row_max + jnp.log(row_total)
        p_low = (weights / row_total).astype(jnp.bfloat16)
        attended = jnp.einsum(
            "shqk,skhe->sqhe", p_low, value_rows, preferred_element_type=jnp.float32
        )
        attended_low = attended.reshape(tokens, heads_local * HD).astype(jnp.bfloat16)
        attention_part = times_transposed(attended_low, full_out)
        upstream_full = out_grad[batch_index].reshape(tokens, model_width).astype(jnp.float32)
        attention_total = reduce_rows(attention_part)
        first_sum = x_full + attention_total + shift_rows[:, 0]
        first_norm, first_back = jax.vjp(norm_rows, first_sum, gain_rows[:, 0], shift_rows[:, 1])
        norm_low = first_norm.astype(jnp.bfloat16)
        before_act = jnp.dot(norm_low, full_up, preferred_element_type=jnp.float32) + up_bias
        activated, gelu_back = jax.vjp(exact_gelu, before_act)
        hidden = activated.astype(jnp.bfloat16)
        down_part = times_transposed(hidden, full_down)
        down_total = reduce_rows(down_part)
        second_sum = first_norm + down_total + shift_rows[:, 2]
        result, second_back = jax.vjp(norm_rows, second_sum, gain_rows[:, 1], shift_rows[:, 3])
        layer_rows.append(pick_rows(result).astype(jnp.bfloat16))
        second_grad, gain_two, shift_three = second_back(upstream_full)
        shift_two = jnp.sum(second_grad, axis=0)
        second_low = second_grad.astype(jnp.bfloat16)
        down_step = contract_rows(second_low, hidden)
        hidden_grad = jnp.dot(second_low, full_down, preferred_element_type=jnp.float32)
        (act_grad,) = gelu_back(hidden_grad)
        up_bias_grad = up_bias_grad + jnp.sum(act_grad, axis=0)
        act_low = act_grad.astype(jnp.bfloat16)
        up_step = contract_rows(norm_low, act_low)
        back_part = times_transposed(act_low, full_up)
        back_total = reduce_rows(back_part)
        norm_grad = second_grad + back_total
        first_grad, gain_one, shift_one = first_back(norm_grad)
        shift_zero = jnp.sum(first_grad, axis=0)
        first_low = first_grad.astype(jnp.bfloat16)
        out_step = contract_rows(first_low, attended_low)
        attended_grad = jnp.dot(first_low, full_out, preferred_element_type=jnp.float32)
        attended_grad = attended_grad.astype(jnp.bfloat16).reshape(
            seq_local, rows_local, heads_local, HD
        )
        scores = masked_scores(queries, key_rows, same_segment, score_scale)
        probabilities = jnp.exp(scores - log_total)
        value_grad = jnp.einsum(
            "shqk,sqhe->skhe",
            probabilities.astype(jnp.bfloat16),
            attended_grad,
            preferred_element_type=jnp.float32,
        )
        prob_grad = jnp.einsum(
            "sqhe,skhe->shqk", attended_grad, value_rows, preferred_element_type=jnp.float32
        )
        row_dot = jnp.sum(prob_grad * probabilities, axis=-1, keepdims=True)
        score_grad = (probabilities * (prob_grad - row_dot)).astype(jnp.bfloat16)
        query_grad = (
            jnp.einsum("shqk,skhe->sqhe", score_grad, key_rows, preferred_element_type=jnp.float32)
            * score_scale
        )
        key_grad = (
            jnp.einsum("shqk,sqhe->skhe", score_grad, queries, preferred_element_type=jnp.float32)
            * score_scale
        )
        kv_grads = lax.psum_scatter(
            jnp.concatenate([key_grad, value_grad], axis=-1).astype(jnp.bfloat16),
            "ctx",
            scatter_dimension=1,
            tiled=True,
        ).astype(jnp.float32)
        key_mine = kv_grads[..., :HD]
        value_mine = kv_grads[..., HD:]
        bias_step = jnp.stack(
            [jnp.sum(query_grad, axis=(0, 1)), jnp.sum(value_mine, axis=(0, 1))], axis=1
        )
        qv_bias_grad = qv_bias_grad + bias_step.reshape(-1)
        mixed_grad = jnp.stack([query_grad, key_mine, value_mine], axis=3)
        mixed_grad = mixed_grad.reshape(tokens, 3 * heads_local * HD).astype(jnp.bfloat16)
        qkv_step = contract_rows(x_low, mixed_grad)
        input_part = times_transposed(mixed_grad, full_qkv).reshape(
            seq_local, rows_local, model_width
        )
        input_mine = lax.psum_scatter(
            input_part.astype(jnp.bfloat16), "tp", scatter_dimension=1, tiled=True
        ).astype(jnp.float32)
        first_part = pick_rows(first_grad)
        input_rows.append(input_mine + first_part)
        gain_step = jnp.stack([gain_one, gain_two], axis=1)
        shift_step = jnp.stack([shift_zero, shift_one, shift_two, shift_three], axis=1)
        full_totals = tuple(
            map(
                add_pair,
                full_totals,
                (qkv_step, out_step, up_step, down_step, gain_step, shift_step),
            )
        )
    share_totals = (
        lax.psum_scatter(
            full_totals[0].astype(jnp.bfloat16), ("fsdp", "ctx"), scatter_dimension=0, tiled=True
        ).astype(jnp.float32),
        lax.psum_scatter(
            full_totals[1].astype(jnp.bfloat16), ("fsdp", "ctx"), scatter_dimension=0, tiled=True
        ).astype(jnp.float32),
        lax.psum_scatter(
            full_totals[2].astype(jnp.bfloat16), ("fsdp", "ctx"), scatter_dimension=0, tiled=True
        ).astype(jnp.float32),
        lax.psum_scatter(
            full_totals[3].astype(jnp.bfloat16), ("fsdp", "ctx"), scatter_dimension=0, tiled=True
        ).astype(jnp.float32),
        lax.psum_scatter(
            full_totals[4].astype(jnp.bfloat16), ("fsdp", "ctx"), scatter_dimension=0, tiled=True
        ).astype(jnp.float32),
        lax.psum_scatter(
            full_totals[5].astype(jnp.bfloat16), ("fsdp", "ctx"), scatter_dimension=0, tiled=True
        ).astype(jnp.float32),
    )
    qv_total, up_total = lax.psum((qv_bias_grad, up_bias_grad), ("fsdp", "ctx"))
    return (
        jnp.stack(layer_rows, axis=0),
        jnp.stack(input_rows, axis=0),
        share_totals[0],
        qv_total,
        share_totals[1],
        share_totals[2],
        up_total,
        share_totals[3],
        share_totals[4],
        share_totals[5],
    )


MESH = pl.DeviceIdType.MESH
ROW_A, ROW_D, ROW_AD, ROW_B = (0, 48), (48, 48), (0, 96), (96, 32)

class Where:
    def __init__(self):
        fsdp = lax.axis_index("fsdp")
        self.y = fsdp // 2
        self.e = fsdp % 2
        self.c = lax.axis_index("ctx")
        self.t = lax.axis_index("tp")
    def at(self, y=None, e=None, c=None, t=None):
        y = self.y if y is None else y
        e = self.e if e is None else e
        c = self.c if c is None else c
        t = self.t if t is None else t
        return (2 * y + e, c, t)

def when(cond, fn):
    if cond is True:
        fn()
    else:
        pl.when(cond)(fn)

class Net:
    def __init__(self, send_sems, recv_sems):
        self.send_sems, self.recv_sems, self.count, self.pending = send_sems, recv_sems, 0, []
    def pair(self):
        self.count += 1
        return self.count - 1
    def send(self, index, cond, src, dst, device):
        def make():
            return pltpu.make_async_remote_copy(
                src_ref=src(), dst_ref=dst(), send_sem=self.send_sems.at[index],
                recv_sem=self.recv_sems.at[index], device_id=device, device_id_type=MESH)
        when(cond, lambda: make().start())
        self.pending.append((cond, make))
    def recv(self, index, cond, here, device):
        def wait():
            pltpu.make_async_remote_copy(
                src_ref=here(), dst_ref=here(), send_sem=self.send_sems.at[index],
                recv_sem=self.recv_sems.at[index], device_id=device, device_id_type=MESH).wait_recv()
        when(cond, wait)
    def drain(self):
        for cond, make in self.pending:
            when(cond, lambda make=make: make().wait_send())

def slots_of(w):
    t = w.t
    return [("own", t, True), ("l1", t - 1, t >= 1), ("r1", t + 1, t <= 2), ("l2", t - 2, t >= 2),
            ("r2", t + 2, t <= 1), ("l3", t - 3, t >= 3), ("r3", t + 3, t <= 0)]

class Gather:
    STAGES = 7
    def __init__(self, net, w, sources, full, c0, cn, local_sems, routes=(ROW_A, ROW_D, ROW_AD, ROW_B)):
        self.net, self.w, self.sources, self.full, self.local_sems = net, w, sources, full, local_sems
        self.cols = pl.ds(c0, cn)
        self.row_a, self.row_d, self.row_ad, self.row_b = [None if r is None else pl.ds(*r) for r in routes]
        self.slots = slots_of(w)
        self.ids = {}
    def id(self, key):
        if key not in self.ids:
            self.ids[key] = self.net.pair()
        return self.ids[key]
    def blk(self, tt, rows, y=None, c=None):
        w = self.w
        y = w.y if y is None else y
        c = w.c if c is None else c
        return lambda: self.full.at[tt, y, :, c, rows, self.cols]
    def row(self, tt, rows, y=None):
        y = self.w.y if y is None else y
        return lambda: self.full.at[tt, y, :, :, rows, self.cols]
    def colm(self, tt, rows, c=None):
        c = self.w.c if c is None else c
        return lambda: self.full.at[tt, :, :, c, rows, self.cols]
    def plane(self, tt, rows):
        return lambda: self.full.at[tt, :, :, :, rows, self.cols]
    def same(self, key, cond, ref, device):
        self.net.send(self.id(key), cond, ref, ref, device)
    def sib(self):
        w = self.w
        self.own_copies = []
        for n, (src, c0, cn) in enumerate(self.sources):
            dst = lambda c0=c0, cn=cn: self.full.at[w.t, w.y, w.e, w.c, :, pl.ds(c0, cn)]
            self.net.send(self.id(("sib", n)), True, lambda src=src: src(1 - w.e), dst, w.at(e=1 - w.e))
            self.own_copies.append(pltpu.make_async_copy(src(w.e), dst(), self.local_sems[n]))
            self.own_copies[-1].start()
    def sib_done(self):
        w = self.w
        for n, (src, c0, cn) in enumerate(self.sources):
            self.own_copies[n].wait()
            self.net.recv(self.id(("sib", n)), True, lambda c0=c0, cn=cn: self.full.at[w.t, w.y, 1 - w.e, w.c, :, pl.ds(c0, cn)], w.at(e=1 - w.e))
    def zsend(self, tag, slot, ref):
        w = self.w
        k = {"own": 0, "l1": 1, "r1": 1, "l2": 2, "r2": 2}[slot]
        if slot == "own" or slot[0] == "l":
            name, tt, ok = self.slot("own" if k == 0 else f"l{k}")
            self.same((tag, "zr", k), (w.t < 3) if ok is True else jnp.logical_and(ok, w.t < 3), ref(tt), w.at(t=w.t + 1))
        if slot == "own" or slot[0] == "r":
            name, tt, ok = self.slot("own" if k == 0 else f"r{k}")
            self.same((tag, "zl", k), (w.t > 0) if ok is True else jnp.logical_and(ok, w.t > 0), ref(tt), w.at(t=w.t - 1))
    def zrecv(self, tag, slot, ref):
        w = self.w
        k = int(slot[1])
        _, tt, ok = self.slot(slot)
        if slot[0] == "l":
            self.net.recv(self.id((tag, "zr", k - 1)), ok, ref(tt), w.at(t=w.t - 1))
        else:
            self.net.recv(self.id((tag, "zl", k - 1)), ok, ref(tt), w.at(t=w.t + 1))
    def slot(self, name):
        return next(s for s in self.slots if s[0] == name)
    def first_hop(self, name):
        w = self.w
        _, tt, ok = self.slot(name)
        self.same(("ax", name), ok, self.blk(tt, self.row_a), w.at(c=1 - w.c))
        if self.row_d is not None:
            self.same(("dy", name), ok, self.blk(tt, self.row_d), w.at(y=1 - w.y))
    def second_hop(self, name):
        w = self.w
        _, tt, ok = self.slot(name)
        self.net.recv(self.id(("ax", name)), ok, self.blk(tt, self.row_a, c=1 - w.c), w.at(c=1 - w.c))
        self.same(("ay", name), ok, self.row(tt, self.row_a), w.at(y=1 - w.y))
        if self.row_d is not None:
            self.net.recv(self.id(("dy", name)), ok, self.blk(tt, self.row_d, y=1 - w.y), w.at(y=1 - w.y))
            self.same(("dx", name), ok, self.colm(tt, self.row_d), w.at(c=1 - w.c))
    def last(self, name):
        w = self.w
        _, tt, ok = self.slot(name)
        self.net.recv(self.id(("ay", name)), ok, self.row(tt, self.row_a, y=1 - w.y), w.at(y=1 - w.y))
        if self.row_d is not None:
            self.net.recv(self.id(("dx", name)), ok, self.colm(tt, self.row_d, c=1 - w.c), w.at(c=1 - w.c))
    def stage(self, k):
        w = self.w
        ad = lambda tt: self.blk(tt, self.row_ad)
        bz = lambda tt: self.plane(tt, self.row_b)
        b = self.row_b is not None
        if k == 0:
            self.sib()
        elif k == 1:
            self.sib_done()
            self.zsend("ad", "own", ad)
            if b:
                self.same("bx", True, self.blk(w.t, self.row_b), w.at(c=1 - w.c))
            self.first_hop("own")
        elif k == 2:
            if b:
                self.net.recv(self.id("bx"), True, self.blk(w.t, self.row_b, c=1 - w.c), w.at(c=1 - w.c))
                self.same("by", True, self.row(w.t, self.row_b), w.at(y=1 - w.y))
            for s in ("l1", "r1"):
                self.zrecv("ad", s, ad)
                self.zsend("ad", s, ad)
                self.first_hop(s)
            self.second_hop("own")
        elif k == 3:
            if b:
                self.net.recv(self.id("by"), True, self.row(w.t, self.row_b, y=1 - w.y), w.at(y=1 - w.y))
                self.zsend("b", "own", bz)
            for s in ("l2", "r2"):
                self.zrecv("ad", s, ad)
                self.zsend("ad", s, ad)
                self.first_hop(s)
            for s in ("l1", "r1"):
                self.second_hop(s)
        elif k == 4:
            if b:
                for s in ("l1", "r1"):
                    self.zrecv("b", s, bz)
                    self.zsend("b", s, bz)
            for s in ("l3", "r3"):
                self.zrecv("ad", s, ad)
                self.first_hop(s)
            for s in ("l2", "r2"):
                self.second_hop(s)
        elif k == 5:
            if b:
                for s in ("l2", "r2"):
                    self.zrecv("b", s, bz)
                    self.zsend("b", s, bz)
            for s in ("l3", "r3"):
                self.second_hop(s)
        elif k == 6:
            if b:
                for s in ("l3", "r3"):
                    self.zrecv("b", s, bz)
            for name, _, _ in self.slots:
                self.last(name)

def barrier(w, extra=()):
    sem = pltpu.get_barrier_semaphore()
    one = lambda dev: pl.semaphore_signal(sem, inc=1, device_id=dev, device_id_type=MESH)
    one(w.at(e=1 - w.e)); one(w.at(c=1 - w.c)); one(w.at(y=1 - w.y))
    pl.when(w.t > 0)(lambda: one(w.at(t=w.t - 1)))
    pl.when(w.t < 3)(lambda: one(w.at(t=w.t + 1)))
    ends = jnp.where(w.t == 0, 1, 0) + jnp.where(w.t == 3, 1, 0)
    return sem, one, 5 - ends

PIECES = ((0, 384), (384, 128), (512, 512), (1024, 512))


def mm(left, right, dims):
    return lax.dot_general(left, right, (dims, ((), ())), preferred_element_type=jnp.float32)


def gather_kernel(
    w_qkv, w_out, w_up, w_down, small, x_in, g_in, ids_col, ids_row,
    full_out, small_out, x_all, g_own, q_out, k_out, v_out, p_out, att_out, sum_out, norm_all, hid_out, dgelu_out,
    full, small_full, att_s, part, land, send_sems, recv_sems, local_sems,
):
    w = Where()
    sem, one, need = barrier(w)
    cross = w.e != w.c
    diag = w.at(e=1 - w.e, c=1 - w.c)
    sibling = w.at(e=1 - w.e)
    pl.when(cross)(lambda: one(diag))
    pl.semaphore_wait(sem, need + jnp.where(cross, 1, 0))
    net = Net(send_sems, recv_sems)
    bf, f32 = jnp.bfloat16, jnp.float32
    seq = lambda ref: ref.at[w.t // 2, w.t % 2]
    def source(ref, i):
        c0, cn = PIECES[i]
        return (lambda e: ref.at[:, pl.ds(pl.multiple_of(e * cn, 128), cn)]), c0, cn
    lo = lambda n: local_sems.at[n]
    tiny = Gather(net, w, [(lambda e: small.at[e], 0, 128)], small_full, 0, 128, [lo(0)], routes=((0, 16), None, (0, 16), None))
    parts = [
        Gather(net, w, [source(w_qkv, 0), source(w_out, 1)], full, 0, 512, [lo(1), lo(2)]),
        Gather(net, w, [source(w_up, 2)], full, 512, 512, [lo(3)]),
        Gather(net, w, [source(w_down, 3)], full, 1024, 512, [lo(4)]),
    ]
    xi, gi, xs, ps, ns = [net.pair() for _ in range(5)]
    parts[0].stage(0)
    tiny.stage(0)
    for idx, src, dst in ((xi, x_in, x_all.at[0]), (gi, g_in, g_own)):
        net.send(idx, cross, lambda src=src: seq(src), lambda dst=dst: dst, diag)
    local = [pltpu.make_async_copy(seq(x_in), x_all.at[0], lo(5)), pltpu.make_async_copy(seq(g_in), g_own, lo(6))]
    for cp in local:
        pl.when(jnp.logical_not(cross))(lambda cp=cp: cp.start())
    parts[1].stage(0)
    parts[2].stage(0)
    parts[0].stage(1)
    tiny.stage(1)
    pl.when(jnp.logical_not(cross))(lambda: local[0].wait())
    net.recv(xi, cross, lambda: x_all.at[0], diag)
    net.send(xs, True, lambda: x_all.at[0], lambda: x_all.at[1], sibling)

    half = x_all.shape[1]
    tokens = 2 * half
    def norm_row(k):
        rows = small_full[0, :, :, :, pl.ds(k, 1), :].astype(f32).reshape(8, 128)
        return jnp.concatenate([rows[i : i + 1] for i in range(8)], axis=1)
    def bias_row(tt, k, n):
        rows = small_full[tt, 0, 0, 0].astype(f32)
        return jnp.concatenate([rows[k + i : k + i + 1] for i in range(n)], axis=1)
    def weight(tt, i):
        return full[tt, :, :, :, :, pl.ds(*PIECES[i])].reshape(1024, PIECES[i][1])
    def qkv(tt):
        x = x_all[...].reshape(tokens, 1024)
        proj = (mm(x, weight(tt, 0), ((1,), (0,))) + bias_row(tt, 6, 3)).astype(bf)
        for h in range(2):
            for n, ref in enumerate((q_out, k_out, v_out)):
                ref[2 * tt + h] = proj[:, (3 * h + n) * HD : (3 * h + n + 1) * HD]
    def attend(tt):
        def body(n, carry):
            h = 2 * tt + n // 2
            rows = pl.ds(pl.multiple_of((n % 2) * half, half), half)
            scores = mm(q_out[h, rows, :], k_out[h], ((1,), (1,))) * (HD ** -0.5)
            scores = jnp.where(ids_col[rows, :] == ids_row[...], scores, masked_score)
            weights = jnp.exp(scores - jnp.max(scores, axis=1, keepdims=True))
            p_low = (weights / jnp.sum(weights, axis=1, keepdims=True)).astype(bf)
            p_out[h, rows, :] = p_low
            att_s[h, rows, :] = mm(p_low, v_out[h], ((1,), (0,))).astype(bf)
            return carry
        lax.fori_loop(0, 4, body, 0)
        att_out[tt] = jnp.concatenate([att_s[2 * tt], att_s[2 * tt + 1]], axis=1)
    def project():
        for n in (1, 0):
            rows = pl.ds(n * half, half)
            total = sum(mm(att_out[tt, rows, :], weight(tt, 1), ((1,), (1,))) for tt in range(4))
            if n == 1:
                part[...] = total.astype(bf)
                net.send(ps, True, lambda: part, lambda: land, sibling)
            else:
                sum_out[...] = total + x_all[0].astype(f32) + norm_row(2)
    def normalize():
        net.recv(ps, True, lambda: land, sibling)
        total = sum_out[...] + land[...].astype(f32)
        sum_out[...] = total
        norm_all[0] = norm_rows(total, norm_row(0), norm_row(3)).astype(bf)
        net.send(ns, True, lambda: norm_all.at[0], lambda: norm_all.at[1], sibling)
    def expand(tt):
        bias = bias_row(tt, 9, 4)
        def body(n, carry):
            before = mm(norm_all[n], weight(tt, 2), ((1,), (0,))) + bias
            rows = pl.ds(pl.multiple_of(n * half, half), half)
            bell = (1.0 + lax.erf(before * (2.0 ** -0.5))) * 0.5
            hid_out[tt, rows, :] = (before * bell).astype(bf)
            slope = bell + before * jnp.exp(before * before * -0.5) * (0.3989422804014327)
            dgelu_out[tt, rows, :] = slope.astype(bf)
            return carry
        lax.fori_loop(0, 2, body, 0)
    def keep(i):
        cols = pl.ds(512 * i, 512)
        cp = pltpu.make_async_copy(full.at[..., cols], full_out.at[..., cols], lo(7 + i))
        cp.start()
        return cp
    kept = []
    for s in range(2, 11):
        if s == 10:
            expand(2)
            expand(3)
        for g, start in ((parts[0], 0), (tiny, 0), (parts[1], 2), (parts[2], 4)):
            if 1 <= s - start <= 6:
                g.stage(s - start)
        if s == 6:
            net.recv(xs, True, lambda: x_all.at[1], sibling)
            for tt in range(4):
                qkv(tt)
            attend(0)
        elif s == 7:
            kept.append(keep(0))
            attend(1)
            attend(2)
        elif s == 8:
            attend(3)
            project()
        elif s == 9:
            kept.append(keep(1))
            normalize()
            net.recv(ns, True, lambda: norm_all.at[1], sibling)
            expand(0)
            expand(1)
    kept.append(keep(2))
    small_out[...] = small_full[...]
    pl.when(jnp.logical_not(cross))(lambda: local[1].wait())
    net.recv(gi, cross, lambda: g_own, diag)
    for cp in kept:
        cp.wait()
    net.drain()

N_GATHER = 156

def run_gather(w_qkv, w_out, w_up, w_down, small, x_in, g_in, ids):
    any_ = pl.BlockSpec(memory_space=pl.ANY)
    vm = pl.BlockSpec(memory_space=pltpu.VMEM)
    rows, width = x_in.shape[2:]
    n = 2 * rows
    bf, f32 = jnp.bfloat16, jnp.float32
    sd = jax.ShapeDtypeStruct
    head = sd((8, n, HD), bf)
    return pl.pallas_call(
        gather_kernel,
        out_shape=(
            sd((4, 2, 2, 2, 128, 1536), bf), sd((4, 2, 2, 2, 16, 128), bf), sd((2, rows, width), bf), sd((rows, width), bf),
            head, head, head, sd((8, n, n), bf), sd((4, n, 128), bf), sd((rows, width), f32), sd((2, rows, width), bf),
            sd((4, n, 512), bf), sd((4, n, 512), bf),
        ),
        in_specs=[any_] * 4 + [vm] + [any_] * 2 + [vm] * 2,
        out_specs=(any_, vm, vm, any_) + (vm,) * 9,
        scratch_shapes=[
            pltpu.VMEM((4, 2, 2, 2, 128, 1536), bf), pltpu.VMEM((4, 2, 2, 2, 16, 128), bf),
            pltpu.VMEM((8, n, HD), bf), pltpu.VMEM((rows, width), bf), pltpu.VMEM((rows, width), bf),
            pltpu.SemaphoreType.DMA((N_GATHER,)), pltpu.SemaphoreType.DMA((N_GATHER,)), pltpu.SemaphoreType.DMA((10,)),
        ],
        compiler_params=pltpu.CompilerParams(collective_id=0, has_side_effects=True),
        name="gather",
    )(w_qkv, w_out, w_up, w_down, small, x_in, g_in, ids[:, None], ids[None, :])


ROWS = {"a": pl.ds(0, 48), "d": pl.ds(48, 48), "ad": pl.ds(0, 96), "b": pl.ds(96, 32)}

class Scatter:
    def __init__(self, net, w, g, bufs, c0, cn):
        self.net, self.w, self.g, self.bufs = net, w, g, bufs
        self.cols = pl.ds(c0, cn)
        self.ids = {}
    def id(self, key):
        if key not in self.ids:
            self.ids[key] = self.net.pair()
        return self.ids[key]
    def take(self, key, cond, buf, place, device):
        cols = self.cols
        def body():
            self.net.recv(self.id(key), True, lambda: buf(), device)
            ref = place()
            ref[...] = (ref[...].astype(jnp.float32) + buf()[...].astype(jnp.float32)).astype(ref.dtype)
        when(cond, body)
    def zstep(self, tag, m, place):
        w = self.w
        for way, me, targets in (("r", m, [j for j in (3, 2, 1) if j >= m]), ("l", 3 - m, [j for j in (0, 1, 2) if j <= 3 - m])):
            buf, step = self.bufs[tag + "z"], 1 if way == "r" else 0
            nxt = w.at(t=w.t + 1) if way == "r" else w.at(t=w.t - 1)
            prv = w.at(t=w.t - 1) if way == "r" else w.at(t=w.t + 1)
            here = w.t == me
            for j in targets:
                land = lambda j=j, buf=buf, step=step: buf.at[j + step, ..., self.cols]
                if m > 0:
                    self.take((tag, way, j), here, land, place(j), prv)
                if j != me:
                    self.net.send(self.id((tag, way, j)), here, place(j), land, nxt)
    def stage(self, k, fill=None):
        w, g, cols, b = self.w, self.g, self.cols, self.bufs
        X, Y = w.at(c=1 - w.c), w.at(y=1 - w.y)
        ad = lambda j: (lambda: g.at[j, w.y, :, w.c, ROWS["ad"], cols])
        bz = lambda j: (lambda: g.at[j, :, :, :, ROWS["b"], cols])
        order = (3, 0, 2, 1)
        if k == 0:
            for j in order:
                fill(j)
                self.net.send(self.id(("ya", j)), True, lambda j=j: g.at[j, 1 - w.y, :, :, ROWS["a"], cols], lambda j=j: b["ya"].at[j, :, :, :, cols], Y)
                self.net.send(self.id(("xd", j)), True, lambda j=j: g.at[j, :, :, 1 - w.c, ROWS["d"], cols], lambda j=j: b["xd"].at[j, :, :, :, cols], X)
            self.zstep("b", 0, bz)
        elif k == 1:
            self.zstep("b", 1, bz)
            for j in order:
                self.take(("ya", j), True, lambda j=j: b["ya"].at[j, :, :, :, cols], lambda j=j: g.at[j, w.y, :, :, ROWS["a"], cols], Y)
                self.net.send(self.id(("xa", j)), True, lambda j=j: g.at[j, w.y, :, 1 - w.c, ROWS["a"], cols], lambda j=j: b["xa"].at[j, :, :, cols], X)
                self.take(("xd", j), True, lambda j=j: b["xd"].at[j, :, :, :, cols], lambda j=j: g.at[j, :, :, w.c, ROWS["d"], cols], X)
                self.net.send(self.id(("yd", j)), True, lambda j=j: g.at[j, 1 - w.y, :, w.c, ROWS["d"], cols], lambda j=j: b["yd"].at[j, :, :, cols], Y)
        elif k == 2:
            self.zstep("b", 2, bz)
            for j in order:
                self.take(("xa", j), True, lambda j=j: b["xa"].at[j, :, :, cols], lambda j=j: g.at[j, w.y, :, w.c, ROWS["a"], cols], X)
                self.take(("yd", j), True, lambda j=j: b["yd"].at[j, :, :, cols], lambda j=j: g.at[j, w.y, :, w.c, ROWS["d"], cols], Y)
            self.zstep("ad", 0, ad)
        elif k == 3:
            self.zstep("b", 3, bz)
            self.net.send(self.id("by"), True, lambda: g.at[w.t, 1 - w.y, :, :, ROWS["b"], cols], lambda: b["by"].at[:, :, :, cols], Y)
            self.zstep("ad", 1, ad)
        elif k == 4:
            self.take("by", True, lambda: b["by"].at[:, :, :, cols], lambda: g.at[w.t, w.y, :, :, ROWS["b"], cols], Y)
            self.net.send(self.id("bx"), True, lambda: g.at[w.t, w.y, :, 1 - w.c, ROWS["b"], cols], lambda: b["bx"].at[:, :, cols], X)
            self.zstep("ad", 2, ad)
        elif k == 5:
            self.zstep("ad", 3, ad)
            self.take("bx", True, lambda: b["bx"].at[:, :, cols], lambda: g.at[w.t, w.y, :, w.c, ROWS["b"], cols], X)
            self.net.send(self.id("sib"), True, lambda: g.at[w.t, w.y, 1 - w.e, w.c, :, cols], lambda: b["sib"].at[:, cols], w.at(e=1 - w.e))
        elif k == 6:
            self.net.recv(self.id("sib"), True, lambda: b["sib"].at[:, cols], w.at(e=1 - w.e))


def scatter_kernel(
    second_low, hidden, norm_low, act_low, first_low, att, q, k, v, p_all, x, first_grad, full, lo, sums,
    o_qkv, o_out, o_up, o_down, lo_out, ig_out, sums_out,
    g, ya, xa, xd, yd, adz, bz, by, bx, sib, sums_run, sums_land, wide, p, agrad, dq, dk, dv, mixed, part, land, ig,
    send_sems, recv_sems, local_sems,
):
    w = Where()
    sem, one, need = barrier(w)
    same = w.e == w.c
    sibling = w.at(e=1 - w.e)
    bf, f32 = jnp.bfloat16, jnp.float32
    for d in range(4):
        go = (lambda d=d: one(w.at(e=w.c, c=w.e, t=(w.t + d) % 4)))
        when(True if d else jnp.logical_not(same), go)
    one(w.at(t=(w.t + 2) % 4))
    pl.semaphore_wait(sem, need + 4 + jnp.where(same, 0, 1))
    net = Net(send_sems, recv_sems)
    bufs = {"ya": ya, "xa": xa, "xd": xd, "yd": yd, "adz": adz, "bz": bz, "by": by, "bx": bx, "sib": sib}
    wide_copy = pltpu.make_async_copy(full.at[..., pl.ds(0, 512)], wide, local_sems.at[0])
    wide_copy.start()
    p_copies = [pltpu.make_async_copy(p_all.at[pl.ds(2 * tt, 2)], p.at[tt % 2], local_sems.at[1 + tt]) for tt in range(4)]
    p_copies[0].start()
    p_copies[1].start()
    down, up, rest = parts = [Scatter(net, w, g, bufs, c0, 512) for c0 in (1024, 512, 0)]

    half = lo.shape[0]
    tokens = 2 * half
    def grads(left, right, i):
        def fill(tt):
            def body(n, carry):
                rows = left[:, pl.ds(pl.multiple_of(n * 256, 256), 256)]
                block = mm(rows, right[tt], ((0,), (0,))).astype(bf)
                g[tt, n // 2, n % 2, :, :, pl.ds(*PIECES[i])] = block.reshape(2, 128, PIECES[i][1])
                return carry
            lax.fori_loop(0, 4, body, 0)
        return fill
    def weight(tt, i):
        return wide[tt, :, :, :, :, pl.ds(*PIECES[i])].reshape(1024, PIECES[i][1])
    def attend_back(tt):
        p_copies[tt].wait()
        upstream = mm(first_low[...], weight(tt, 1), ((1,), (0,))).astype(bf)
        agrad[0] = upstream[:, :HD]
        agrad[1] = upstream[:, HD:]
        dk[...] = jnp.zeros_like(dk)
        dv[...] = jnp.zeros_like(dv)
        def body(n, carry):
            h = n // 2
            head = 2 * tt + h
            rows = pl.ds(pl.multiple_of((n % 2) * half, half), half)
            p_low, above = p[tt % 2, h, rows, :], agrad[h, rows, :]
            prob = p_low.astype(f32)
            prob_grad = mm(above, v[head], ((1,), (1,)))
            row_dot = jnp.sum(prob_grad * prob, axis=1, keepdims=True)
            score_grad = (prob * (prob_grad - row_dot)).astype(bf)
            dq[h, rows, :] = mm(score_grad, k[head], ((1,), (0,)))
            dk[h] += mm(score_grad, q[head, rows, :], ((0,), (0,)))
            dv[h] += mm(p_low, above, ((0,), (0,)))
            return carry
        lax.fori_loop(0, 4, body, 0)
        pieces = []
        for h in range(2):
            query_grad, value_grad = dq[h] * (HD ** -0.5), dv[h]
            pieces += [query_grad, dk[h] * (HD ** -0.5), value_grad]
            row = jnp.concatenate([jnp.sum(query_grad, axis=0, keepdims=True), jnp.sum(value_grad, axis=0, keepdims=True)], axis=1)
            sums_run[0, pl.ds(48 + 8 * w.e + 2 * tt + h, 1), :] = row
        mixed[tt] = jnp.concatenate([a.astype(bf) for a in pieces], axis=1)
        if tt < 2:
            p_copies[tt + 2].start()
    def input_rows(n):
        rows = pl.ds(n * half, half)
        return sum(mm(mixed[tt, rows, :], weight(tt, 0), ((1,), (1,))) for tt in range(4))

    ids = [[net.pair(), net.pair()] for _ in range(4)]
    pi = net.pair()
    def rows_out(kind, src, dst, local):
        for d in range(4):
            t2 = (w.t + d) % 4
            here = lambda t2=t2: src.at[pl.ds(pl.multiple_of(t2 * 64, 64), 64)]
            there = lambda: dst.at[w.t // 2, w.t % 2]
            net.send(ids[d][kind], True if d else jnp.logical_not(same), here, there, w.at(e=w.c, c=w.e, t=t2))
        cp = pltpu.make_async_copy(src.at[pl.ds(pl.multiple_of(w.t * 64, 64), 64)], dst.at[w.t // 2, w.t % 2], local)
        pl.when(same)(lambda: cp.start())
        return cp
    def rows_in(kind, dst):
        for d in range(4):
            t2 = (w.t + 4 - d) % 4
            net.recv(ids[d][kind], True if d else jnp.logical_not(same), lambda t2=t2: dst.at[t2 // 2, t2 % 2], w.at(e=w.c, c=w.e, t=t2))
    partners = (sibling, w.at(c=1 - w.c), w.at(y=1 - w.y), w.at(t=w.t + 1 - 2 * (w.t % 2)), w.at(t=(w.t + 2) % 4))
    sums_ids = [net.pair() for _ in partners]
    def sums_step(s):
        if s > 0:
            net.recv(sums_ids[s - 1], True, lambda: sums_land.at[s - 1], partners[s - 1])
            total = sums_run[s - 1] + sums_land[s - 1]
            if s == 5:
                sums_out[...] = total
            else:
                sums_run[s] = total
        if s < 5:
            net.send(sums_ids[s], True, lambda: sums_run.at[s], lambda: sums_land.at[s], partners[s])
    def finish(*pieces):
        for i in pieces:
            c0, cn = PIECES[i]
            ref = (o_qkv, o_out, o_up, o_down)[i]
            cols = pl.ds(c0, cn)
            ref[:, pl.ds(pl.multiple_of(w.e * cn, 128), cn)] = g[w.t, w.y, w.e, w.c, :, cols].astype(f32)
            ref[:, pl.ds(pl.multiple_of((1 - w.e) * cn, 128), cn)] = sib[:, cols].astype(f32)

    sums_run[0] = sums[...]
    down.stage(0, grads(second_low, hidden, 3))
    up.stage(0, grads(norm_low, act_low, 2))
    own = [rows_out(0, lo, lo_out, local_sems.at[5])]
    wide_copy.wait()
    attend_back(0)
    down.stage(1)
    attend_back(1)
    attend_back(2)
    down.stage(2)
    up.stage(1)
    attend_back(3)
    sums_step(0)
    fill_qkv, fill_out = grads(x, mixed, 0), grads(first_low, att, 1)
    def fill_rest(tt):
        fill_qkv(tt)
        fill_out(tt)
    rest.stage(0, fill_rest)
    sums_step(1)
    down.stage(3)
    up.stage(2)
    part[...] = input_rows(1).astype(bf)
    net.send(pi, True, lambda: part, lambda: land, sibling)
    sums_step(2)
    down.stage(4)
    up.stage(3)
    ig_mine = first_grad[...] + input_rows(0)
    net.recv(pi, True, lambda: land, sibling)
    ig[...] = (ig_mine + land[...].astype(f32)).astype(bf)
    own.append(rows_out(1, ig, ig_out, local_sems.at[6]))
    rest.stage(1)
    sums_step(3)
    down.stage(5)
    up.stage(4)
    rest.stage(2)
    sums_step(4)
    down.stage(6)
    finish(3)
    up.stage(5)
    rest.stage(3)
    up.stage(6)
    finish(2)
    sums_step(5)
    rest.stage(4)
    rest.stage(5)
    rest.stage(6)
    finish(0, 1)
    for cp in own:
        pl.when(same)(lambda cp=cp: cp.wait())
    rows_in(0, lo_out)
    rows_in(1, ig_out)
    net.drain()

N_SCATTER = 107

def run_scatter(second_low, hidden, norm_low, act_low, first_low, att, q, k, v, p_low, x, first_grad, full, lo, sums):
    any_ = pl.BlockSpec(memory_space=pl.ANY)
    vm = pl.BlockSpec(memory_space=pltpu.VMEM)
    f32, bf = jnp.float32, jnp.bfloat16
    n = full.shape[-1]
    rows, width = lo.shape
    tokens = 2 * rows
    share = rows // 4
    sd = jax.ShapeDtypeStruct
    return pl.pallas_call(
        scatter_kernel,
        out_shape=(sd((128, 768), f32), sd((128, 256), f32), sd((128, 1024), f32), sd((128, 1024), f32),
                   sd((2, 2, share, width), bf), sd((2, 2, share, width), bf), sd(sums.shape, f32)),
        in_specs=[vm] * 9 + [any_] + [vm] * 2 + [any_] + [vm] * 2,
        out_specs=(vm, vm, vm, vm, any_, any_, vm),
        scratch_shapes=[pltpu.VMEM((4, 2, 2, 2, 128, n), bf),
                        pltpu.VMEM((4, 2, 2, 48, n), bf), pltpu.VMEM((4, 2, 48, n), bf),
                        pltpu.VMEM((4, 2, 2, 48, n), bf), pltpu.VMEM((4, 2, 48, n), bf),
                        pltpu.VMEM((5, 2, 96, n), bf), pltpu.VMEM((5, 2, 2, 2, 32, n), bf),
                        pltpu.VMEM((2, 2, 32, n), bf), pltpu.VMEM((2, 32, n), bf), pltpu.VMEM((128, n), bf),
                        pltpu.VMEM((5,) + sums.shape, f32), pltpu.VMEM((5,) + sums.shape, f32),
                        pltpu.VMEM((4, 2, 2, 2, 128, 512), bf), pltpu.VMEM((2, 2, tokens, tokens), bf),
                        pltpu.VMEM((2, tokens, HD), bf), pltpu.VMEM((2, tokens, HD), f32), pltpu.VMEM((2, tokens, HD), f32),
                        pltpu.VMEM((2, tokens, HD), f32), pltpu.VMEM((4, tokens, 6 * HD), bf),
                        pltpu.VMEM((rows, width), bf), pltpu.VMEM((rows, width), bf), pltpu.VMEM((rows, width), bf),
                        pltpu.SemaphoreType.DMA((N_SCATTER,)), pltpu.SemaphoreType.DMA((N_SCATTER,)), pltpu.SemaphoreType.DMA((7,))],
        compiler_params=pltpu.CompilerParams(collective_id=1, has_side_effects=True, vmem_limit_bytes=67043328),
        name="scatter",
    )(second_low, hidden, norm_low, act_low, first_low, att, q, k, v, p_low, x, first_grad, full, lo, sums)


def swap_cores(value):
    return lax.ppermute(value, "fsdp", [(i, i ^ 1) for i in range(lax.axis_size("fsdp"))])


def own_rows(part):
    half = part.shape[0] // 2
    return part[:half] + swap_cores(part[half:].astype(jnp.bfloat16)).astype(jnp.float32)


def both_rows(rows_mine):
    return jnp.concatenate([rows_mine, swap_cores(rows_mine)], axis=0)


def dot32(spec, left, right):
    return jnp.einsum(spec, left, right, preferred_element_type=jnp.float32)


def fast_local(
    inputs, out_grad, segment_ids, w_qkv, bias_qv, w_out, w_up, bias_up, w_down, gains, shifts
):
    w = Where()
    bf, f32 = jnp.bfloat16, jnp.float32
    rows, model_width = inputs.shape[2:]
    tokens = 2 * rows
    score_scale = HD ** (-0.5)
    norms_in = jnp.concatenate([gains, shifts], axis=1).T
    qv = bias_qv.reshape(2, 2, 2, HD)
    qkv_bias = jnp.stack([qv[:, :, 0], jnp.zeros_like(qv[:, :, 0]), qv[:, :, 1]], axis=2)
    small = jnp.concatenate(
        [
            jnp.broadcast_to(norms_in, (2, 6, 128)),
            qkv_bias.reshape(2, 3, 128),
            bias_up.reshape(2, 4, 128),
            jnp.zeros((2, 3, 128), bf),
        ],
        axis=1,
    )
    ids = jnp.where(w.e == w.c, segment_ids, swap_cores(segment_ids)).reshape(4, 2, rows)
    ids = lax.dynamic_index_in_dim(ids, w.t, 0, keepdims=False)
    ids = jnp.where(w.e == 0, ids, ids[::-1]).reshape(tokens)
    (
        full_all, small_full, x_all, upstream, queries, key_rows, value_rows, p_low, attended_low,
        first_sum, norm_low, hidden, gelu_slope,
    ) = run_gather(w_qkv, w_out, w_up, w_down, small, inputs, out_grad, ids)
    full = full_all.reshape(4, model_width, -1)
    small_full = small_full.reshape(4, 8, 16, 128)
    norm_all = small_full[0, :, :6].transpose(1, 0, 2).reshape(6, model_width).astype(f32)
    gain_rows, shift_rows = norm_all[:2], norm_all[2:]
    full_up, full_down = (full[:, :, c0 : c0 + cn] for c0, cn in PIECES[2:])
    x_low = x_all.reshape(tokens, model_width)
    norm_low = norm_low.reshape(tokens, model_width)
    first_norm, first_back = jax.vjp(norm_rows, first_sum, gain_rows[0], shift_rows[1])
    down_part = dot32("tnc,tkc->nk", hidden, full_down)
    second_sum = first_norm + own_rows(down_part) + shift_rows[2]
    result, second_back = jax.vjp(norm_rows, second_sum, gain_rows[1], shift_rows[3])
    layer_mine = result.astype(bf)
    second_grad, gain_two, shift_three = second_back(upstream.astype(f32))
    shift_two = jnp.sum(second_grad, axis=0)
    second_low = both_rows(second_grad.astype(bf))
    hidden_grad = dot32("nk,tkc->tnc", second_low, full_down)
    act_grad = hidden_grad * gelu_slope.astype(f32)
    up_bias_grad = jnp.sum(act_grad, axis=1)
    act_low = act_grad.astype(bf)
    back_part = dot32("tnc,tkc->nk", act_low, full_up)
    norm_grad = second_grad + own_rows(back_part)
    first_grad, gain_one, shift_one = first_back(norm_grad)
    shift_zero = jnp.sum(first_grad, axis=0)
    first_low = both_rows(first_grad.astype(bf))
    norm_sums = jnp.stack([gain_one, gain_two, shift_zero, shift_one, shift_two, shift_three])
    up_sums = jnp.stack([jnp.where(w.e == i, up_bias_grad, 0.0) for i in range(2)])
    sums = jnp.concatenate(
        [norm_sums.reshape(48, 128), jnp.zeros((16, 128), f32), up_sums.reshape(32, 128)]
    )
    g_qkv, g_out, g_up, g_down, layer_out, input_out, sums = run_scatter(
        second_low, hidden, norm_low, act_low, first_low, attended_low, queries, key_rows,
        value_rows, p_low, x_low, first_grad, full_all, layer_mine, sums,
    )
    qv_mine = lax.dynamic_index_in_dim(sums[48:64].reshape(2, 4, 256), w.t, 1, keepdims=False)
    up_mine = lax.dynamic_index_in_dim(sums[64:].reshape(2, 4, 512), w.t, 1, keepdims=False)
    block = (2 * w.y + w.e) * 2 + w.c
    norm_mine = lax.dynamic_index_in_dim(sums[:48].reshape(6, 8, 128), block, 1, keepdims=False)
    return (
        layer_out,
        input_out.astype(f32),
        g_qkv,
        qv_mine.reshape(-1),
        g_out,
        g_up,
        up_mine.reshape(-1),
        g_down,
        norm_mine[:2].T,
        norm_mine[2:].T,
    )


def fits_fast(mesh):
    return dict(mesh.shape) == {"fsdp": 4, "ctx": 2, "tp": 4}


def solution(mesh):
    placed = (
        P(None, "fsdp", "ctx", None),
        P(None, "fsdp", "ctx", None),
        P(None, "fsdp", None),
        P(("fsdp", "ctx"), "tp"),
        P("tp"),
        P(("fsdp", "ctx"), "tp"),
        P(("fsdp", "ctx"), "tp"),
        P("tp"),
        P(("fsdp", "ctx"), "tp"),
        P(("fsdp", "ctx"), None),
        P(("fsdp", "ctx"), None),
    )
    return jax.shard_map(
        fast_local if fits_fast(mesh) else local,
        mesh=mesh,
        in_specs=placed,
        out_specs=(
            P(None, "fsdp", ("ctx", "tp"), None),
            P(None, "fsdp", ("ctx", "tp"), None),
            P(("fsdp", "ctx"), "tp"),
            P("tp"),
            P(("fsdp", "ctx"), "tp"),
            P(("fsdp", "ctx"), "tp"),
            P("tp"),
            P(("fsdp", "ctx"), "tp"),
            P(("fsdp", "ctx"), None),
            P(("fsdp", "ctx"), None),
        ),
        check_vma=False,
    )
```

profile of v0, /device:TPU:0, one launch (start us, length us, event | category | flops | bytes accessed | tf_op | source)
XLA Modules:
  0.0 311.7 jit_solution(11877178575485572768)
XLA Ops:
  1.2 0.8 reshape.171
  3.0 1.4 maximum_maximum_fusion.small
  5.2 0.9 copy.28
  6.1 117.3 %gather.1 = (bf16[4,2,2,2,128,1536]{5,4,3,2,1,0:T(8,128)(2,1)}, bf16[4,2,2,2,16,128]{5,4,3,2,1,0:T(8,128)(2,1)}, bf16[2,256,1024]{2,1,0:T(8,128)(2,1)}, bf16[256...) custom-call(bf16[128,768]{1,0:T(8,128)(2,1)} %w_qkv.1, ...), custom_call_target="tpu_custom_call" | custom-call | tf_op jit(solution)/shard_map/gather/pallas_call | solution.py:596
  123.4 1.5 reduce_sum.132
  124.9 1.5 multiply_reduce_fusion.3
  126.4 4.7 %fusion.8 = f32[512,1024]{1,0:T(8,128)S(1)} fusion(bf16[4,512,512]{2,1,0:T(8,128)(2,1)S(1)} %copy-done.2, bf16[4,1024,1536]{2,1,0:T(8,128)(2,1)} %bitcast.73), kind=kOutput, calls=%fused_computation.9 | convolution fusion | flops 2147483648 | bytes 8388608 | tf_op jit(solution)/shard_map/tnc,tkc->nk/dot_general | solution.py:894
  132.0 1.1 collective-permute-done.1
  134.2 1.2 fusion.17
  136.3 1.8 collective-permute-done.2
  138.1 2.4 fusion.6
  140.5 2.4 fusion.11
  142.9 1.0 slice.136
  144.6 1.9 collective-permute-done.3
  146.5 1.9 multiply_reduce_fusion
  149.0 1.0 copy-done.1
  150.3 1.0 pad_maximum_fusion.second_low
  152.1 1.0 pad_maximum_fusion.1.first_low
  153.2 147.9 %scatter.1 = (f32[128,768]{1,0:T(8,128)}, f32[128,256]{1,0:T(8,128)}, f32[128,1024]{1,0:T(8,128)}, f32[128,1024]{1,0:T(8,128)}, bf16[2,2,64,1024]{3,2,1,0:T(8,12...) custom-call(bf16[512,1024]{1,0:T(8,128)(2,1)} %pad_maximum_fusion.second_low, ...), custom_call_target="tpu_custom_call" | custom-call | tf_op jit(solution)/shard_map/scatter/pallas_call | solution.py:858
  301.1 0.9 slice_bitcast_fusion
  303.4 2.2 convert_element_type.50
  307.9 0.8 copy.35
  310.1 0.8 copy.38
  310.9 0.8 copy.39
  (93 shorter events, 12.8 us)
Async XLA Ops:
  0.6 3.7 %collective-permute-start = (s32[2,2,512]{2,1,0:T(2,128)}, s32[2,2,512]{2,1,0:T(2,128)S(1)}, u32[]{:S(2)}, u32[]{:S(2)}) collective-permute-start(s32[2,2,512]{2,1,0:T(2,128)} %param.13), channel_id=1, source_target_pairs={{0,8},{8,0},{16,24},{24,16},{1,9},{9,1},{17,25},{25,17},{2,10},{10... | collective-permute-start | bytes 24584 | tf_op jit(solution)/shard_map/ppermute | solution.py:881
  5.2 0.9 copy-start.13
  123.4 3.0 copy-start.2
  126.4 6.8 %copy-start = (f32[256,1024]{1,0:T(8,128)S(1)}, f32[256,1024]{1,0:T(8,128)}, u32[]{:S(2)}) copy-start(f32[256,1024]{1,0:T(8,128)} %get-tuple-element.32) | copy-start | bytes 3145732
  126.4 11.7 %slice-start = ((s8[12582912]{0:T(1024)(128)(4,1)}), s8[4194304]{0:T(1024)(128)(4,1)S(1)}, s32[]{:S(2)}) async-start(s8[12582912]{0:T(1024)(128)(4,1)} %bitcast.74), calls=%async_computation | async-start | bytes 8388608
  126.4 11.7 %slice-start.1 = ((s8[12582912]{0:T(1024)(128)(4,1)}), s8[4194304]{0:T(1024)(128)(4,1)S(1)}, s32[]{:S(2)}) async-start(s8[12582912]{0:T(1024)(128)(4,1)} %bitcast.74), calls=%async_computation.1 | async-start | bytes 8388608
  131.2 2.0 collective-permute-start.1
  133.2 1.0 copy-start.4
  133.2 4.9 %slice-start.2 = ((s8[12582912]{0:T(1024)(128)(4,1)}), s8[4194304]{0:T(1024)(128)(4,1)S(1)}, s32[]{:S(2)}) async-start(s8[12582912]{0:T(1024)(128)(4,1)} %bitcast.74), calls=%async_computation.2 | async-start | bytes 8388608
  135.5 2.6 copy-start.14
  136.1 2.0 collective-permute-start.2
  138.1 2.4 copy-start.9
  140.5 2.4 copy-start.3
  142.9 1.5 copy-start.5
  144.4 2.1 collective-permute-start.3
  148.8 1.5 copy-start.10
  149.0 1.0 copy-start.1
  150.1 2.1 collective-permute-start.4
  301.1 6.9 %copy-start.8 = (bf16[2,2,64,1024]{3,2,1,0:T(8,128)(2,1)S(1)}, bf16[2,2,64,1024]{3,2,1,0:T(8,128)(2,1)}, u32[]{:S(2)}) copy-start(bf16[2,2,64,1024]{3,2,1,0:T(8,128)(2,1)} %get-tuple-element.89) | copy-start | bytes 1572868
  301.1 7.6 %copy-start.11 = (f32[128,768]{1,0:T(8,128)S(1)}, f32[128,768]{1,0:T(8,128)}, u32[]{:S(2)}) copy-start(f32[128,768]{1,0:T(8,128)} %get-tuple-element.91) | copy-start | bytes 1179652
  301.1 8.4 %copy-start.12 = (f32[128,256]{1,0:T(8,128)S(1)}, f32[128,256]{1,0:T(8,128)}, u32[]{:S(2)}) copy-start(f32[128,256]{1,0:T(8,128)} %get-tuple-element.93) | copy-start | bytes 393220
  301.1 9.0 %copy-start.7 = (f32[128,1024]{1,0:T(8,128)S(1)}, f32[128,1024]{1,0:T(8,128)}, u32[]{:S(2)}) copy-start(f32[128,1024]{1,0:T(8,128)} %get-tuple-element.94) | copy-start | bytes 1572868
  303.4 7.5 %copy-start.6 = (f32[128,1024]{1,0:T(8,128)S(1)}, f32[128,1024]{1,0:T(8,128)}, u32[]{:S(2)}) copy-start(f32[128,1024]{1,0:T(8,128)} %get-tuple-element.96) | copy-start | bytes 1572868
where the time goes:
time: 312 us
  Pallas kernels  265 us (85%)
  other arithmetic  16.7 us (5%)
  local copies, waits for them, and re-layouts  13.5 us (4%)
  matrix products  9.42 us (3%)
  waiting for transfers between devices  4.83 us (2%)
    pallas_call x1, Pallas kernels, run_scatter(): pl.pallas_call(scatter_kernel, out_shape=(sd((128, 768), f32), sd((128, 2...  148 us
    pallas_call x1, Pallas kernels, run_gather(): pl.pallas_call(gather_kernel, out_shape=(sd((4, 2, 2, 2, 128, 1536), bf),...  117 us
    dot_general x3, matrix products, dot32(): return jnp.einsum(spec, left, right, preferred_element_type=jnp.float32)  9.42 us
    unnamed x43, local copies, waits for them, and re-layouts  6.51 us
  transfers between devices with their start and end apart: 5, of which 3 were waited for; matrix products, arithmetic and copies ran while one was open for 2% of the time, Pallas kernels for 0%

commit v1 on v0

--- a/solution.py
+++ b/solution.py
@@ -685,9 +685,9 @@
 
 
 def scatter_kernel(
-    second_low, hidden, norm_low, act_low, first_low, att, q, k, v, p_all, x, first_grad, full, lo, sums,
+    second_low, hidden, norm_low, slope_all, att, q, k, v, p_all, x, first_sum, second_grad, gain, full, lo, sums,
     o_qkv, o_out, o_up, o_down, lo_out, ig_out, sums_out,
-    g, ya, xa, xd, yd, adz, bz, by, bx, sib, sums_run, sums_land, wide, p, agrad, dq, dk, dv, mixed, part, land, ig,
+    g, ya, xa, xd, yd, adz, bz, by, bx, sib, sums_run, sums_land, wide, stream, slope, act_low, first_low, first_grad, back, agrad, dq, dk, dv, mixed, part, land, part_two, land_two, ig,
     send_sems, recv_sems, local_sems,
 ):
     w = Where()
@@ -704,9 +704,16 @@
     bufs = {"ya": ya, "xa": xa, "xd": xd, "yd": yd, "adz": adz, "bz": bz, "by": by, "bx": bx, "sib": sib}
     wide_copy = pltpu.make_async_copy(full.at[..., pl.ds(0, 512)], wide, local_sems.at[0])
     wide_copy.start()
-    p_copies = [pltpu.make_async_copy(p_all.at[pl.ds(2 * tt, 2)], p.at[tt % 2], local_sems.at[1 + tt]) for tt in range(4)]
-    p_copies[0].start()
-    p_copies[1].start()
+    order = (3, 0, 2, 1)
+    sources = [full.at[tt, :, :, :, :, pl.ds(*PIECES[3])] for tt in order] + [full.at[tt, :, :, :, :, pl.ds(*PIECES[2])] for tt in range(4)]
+    sources += [p_all.at[pl.ds(2 * tt, 2)] for tt in range(4)]
+    loads = [pltpu.make_async_copy(src, stream.at[n % 2], local_sems.at[7 + n]) for n, src in enumerate(sources)]
+    slopes = [pltpu.make_async_copy(slope_all.at[tt], slope.at[n % 2], local_sems.at[1 + n]) for n, tt in enumerate(order)]
+    for cp in loads[:2] + slopes[:2]:
+        cp.start()
+    def used(copies, n):
+        if n + 2 < len(copies):
+            copies[n + 2].start()
     down, up, rest = parts = [Scatter(net, w, g, bufs, c0, 512) for c0 in (1024, 512, 0)]
 
     half = lo.shape[0]
@@ -714,7 +721,7 @@
     def grads(left, right, i):
         def fill(tt):
             def body(n, carry):
-                rows = left[:, pl.ds(pl.multiple_of(n * 256, 256), 256)]
+                rows = left[..., pl.ds(pl.multiple_of(n * 256, 256), 256)].reshape(tokens, 256)
                 block = mm(rows, right[tt], ((0,), (0,))).astype(bf)
                 g[tt, n // 2, n % 2, :, :, pl.ds(*PIECES[i])] = block.reshape(2, 128, PIECES[i][1])
                 return carry
@@ -723,8 +730,8 @@
     def weight(tt, i):
         return wide[tt, :, :, :, :, pl.ds(*PIECES[i])].reshape(1024, PIECES[i][1])
     def attend_back(tt):
-        p_copies[tt].wait()
-        upstream = mm(first_low[...], weight(tt, 1), ((1,), (0,))).astype(bf)
+        loads[8 + tt].wait()
+        upstream = mm(first_low[...].reshape(tokens, 1024), weight(tt, 1), ((1,), (0,))).astype(bf)
         agrad[0] = upstream[:, :HD]
         agrad[1] = upstream[:, HD:]
         dk[...] = jnp.zeros_like(dk)
@@ -733,7 +740,7 @@
             h = n // 2
             head = 2 * tt + h
             rows = pl.ds(pl.multiple_of((n % 2) * half, half), half)
-            p_low, above = p[tt % 2, h, rows, :], agrad[h, rows, :]
+            p_low, above = stream[tt % 2, h, n % 2].reshape(half, tokens), agrad[h, rows, :]
             prob = p_low.astype(f32)
             prob_grad = mm(above, v[head], ((1,), (1,)))
             row_dot = jnp.sum(prob_grad * prob, axis=1, keepdims=True)
@@ -750,14 +757,48 @@
             row = jnp.concatenate([jnp.sum(query_grad, axis=0, keepdims=True), jnp.sum(value_grad, axis=0, keepdims=True)], axis=1)
             sums_run[0, pl.ds(48 + 8 * w.e + 2 * tt + h, 1), :] = row
         mixed[tt] = jnp.concatenate([a.astype(bf) for a in pieces], axis=1)
-        if tt < 2:
-            p_copies[tt + 2].start()
+        used(loads, 8 + tt)
+    def activate(tt):
+        n = order.index(tt)
+        loads[n].wait()
+        slopes[n].wait()
+        hidden_grad = mm(second_low[...], stream[n % 2].reshape(1024, 512), ((1,), (0,)))
+        act_grad = hidden_grad * slope[n % 2].astype(f32)
+        act_low[tt] = act_grad.astype(bf)
+        used(loads, n)
+        used(slopes, n)
+        total = jnp.sum(act_grad, axis=0, keepdims=True)
+        for i in range(4):
+            sums_run[0, pl.ds(64 + 16 * w.e + 4 * tt + i, 1), :] = total[:, 128 * i : 128 * (i + 1)]
+    def go_back():
+        for tt in range(4):
+            loads[4 + tt].wait()
+            product = mm(act_low[tt], stream[tt % 2].reshape(1024, 512), ((1,), (1,)))
+            back[...] = product if tt == 0 else back[...] + product
+            used(loads, 4 + tt)
+        part_two[...] = back[half:, :].astype(bf)
+        net.send(pb, True, lambda: part_two, lambda: land_two, sibling)
+    def first_back():
+        net.recv(pb, True, lambda: land_two, sibling)
+        norm_grad = second_grad[...] + (back[:half, :] + land_two[...].astype(f32))
+        centered = first_sum[...] - jnp.mean(first_sum[...], axis=1, keepdims=True)
+        inverse = lax.rsqrt(jnp.mean(centered * centered, axis=1, keepdims=True) + norm_epsilon)
+        unit = centered * inverse
+        slanted = norm_grad * gain[...]
+        grad = inverse * (slanted - jnp.mean(slanted, axis=1, keepdims=True) - unit * jnp.mean(slanted * unit, axis=1, keepdims=True))
+        first_grad[...] = grad
+        first_low[0] = grad.astype(bf)
+        net.send(pf, True, lambda: first_low.at[0], lambda: first_low.at[1], sibling)
+        for at, value in ((0, norm_grad * unit), (16, grad), (24, norm_grad)):
+            total = jnp.sum(value, axis=0, keepdims=True)
+            for i in range(8):
+                sums_run[0, at + i : at + i + 1, :] = total[:, 128 * i : 128 * (i + 1)]
     def input_rows(n):
         rows = pl.ds(n * half, half)
         return sum(mm(mixed[tt, rows, :], weight(tt, 0), ((1,), (1,))) for tt in range(4))
 
     ids = [[net.pair(), net.pair()] for _ in range(4)]
-    pi = net.pair()
+    pi, pb, pf = net.pair(), net.pair(), net.pair()
     def rows_out(kind, src, dst, local):
         for d in range(4):
             t2 = (w.t + d) % 4
@@ -793,49 +834,54 @@
 
     sums_run[0] = sums[...]
     down.stage(0, grads(second_low, hidden, 3))
-    up.stage(0, grads(norm_low, act_low, 2))
+    fill_up = grads(norm_low, act_low, 2)
+    def fill_act(tt):
+        activate(tt)
+        fill_up(tt)
+    up.stage(0, fill_act)
+    go_back()
     own = [rows_out(0, lo, lo_out, local_sems.at[5])]
+    down.stage(1)
+    first_back()
     wide_copy.wait()
-    attend_back(0)
-    down.stage(1)
-    attend_back(1)
-    attend_back(2)
-    down.stage(2)
-    up.stage(1)
-    attend_back(3)
-    sums_step(0)
+    net.recv(pf, True, lambda: first_low.at[1], sibling)
+    for tt in range(4):
+        attend_back(tt)
     fill_qkv, fill_out = grads(x, mixed, 0), grads(first_low, att, 1)
     def fill_rest(tt):
         fill_qkv(tt)
         fill_out(tt)
     rest.stage(0, fill_rest)
-    sums_step(1)
+    up.stage(1)
+    down.stage(2)
+    sums_step(0)
+    part[...] = input_rows(1).astype(bf)
+    net.send(pi, True, lambda: part, lambda: land, sibling)
+    ig_mine = first_grad[...] + input_rows(0)
     down.stage(3)
     up.stage(2)
-    part[...] = input_rows(1).astype(bf)
-    net.send(pi, True, lambda: part, lambda: land, sibling)
-    sums_step(2)
-    down.stage(4)
-    up.stage(3)
-    ig_mine = first_grad[...] + input_rows(0)
+    rest.stage(1)
+    sums_step(1)
     net.recv(pi, True, lambda: land, sibling)
     ig[...] = (ig_mine + land[...].astype(f32)).astype(bf)
     own.append(rows_out(1, ig, ig_out, local_sems.at[6]))
-    rest.stage(1)
-    sums_step(3)
+    down.stage(4)
+    up.stage(3)
+    rest.stage(2)
+    sums_step(2)
     down.stage(5)
     up.stage(4)
-    rest.stage(2)
-    sums_step(4)
+    rest.stage(3)
+    sums_step(3)
     down.stage(6)
     finish(3)
     up.stage(5)
-    rest.stage(3)
+    rest.stage(4)
+    sums_step(4)
     up.stage(6)
     finish(2)
+    rest.stage(5)
     sums_step(5)
-    rest.stage(4)
-    rest.stage(5)
     rest.stage(6)
     finish(0, 1)
     for cp in own:
@@ -844,9 +890,9 @@
     rows_in(1, ig_out)
     net.drain()
 
-N_SCATTER = 107
-
-def run_scatter(second_low, hidden, norm_low, act_low, first_low, att, q, k, v, p_low, x, first_grad, full, lo, sums):
+N_SCATTER = 109
+
+def run_scatter(second_low, hidden, norm_low, slope, att, q, k, v, p_low, x, first_sum, second_grad, gain, full, lo, sums):
     any_ = pl.BlockSpec(memory_space=pl.ANY)
     vm = pl.BlockSpec(memory_space=pltpu.VMEM)
     f32, bf = jnp.float32, jnp.bfloat16
@@ -859,7 +905,7 @@
         scatter_kernel,
         out_shape=(sd((128, 768), f32), sd((128, 256), f32), sd((128, 1024), f32), sd((128, 1024), f32),
                    sd((2, 2, share, width), bf), sd((2, 2, share, width), bf), sd(sums.shape, f32)),
-        in_specs=[vm] * 9 + [any_] + [vm] * 2 + [any_] + [vm] * 2,
+        in_specs=[vm] * 3 + [any_] + [vm] * 4 + [any_] + [vm] * 4 + [any_] + [vm] * 2,
         out_specs=(vm, vm, vm, vm, any_, any_, vm),
         scratch_shapes=[pltpu.VMEM((4, 2, 2, 2, 128, n), bf),
                         pltpu.VMEM((4, 2, 2, 48, n), bf), pltpu.VMEM((4, 2, 48, n), bf),
@@ -867,14 +913,15 @@
                         pltpu.VMEM((5, 2, 96, n), bf), pltpu.VMEM((5, 2, 2, 2, 32, n), bf),
                         pltpu.VMEM((2, 2, 32, n), bf), pltpu.VMEM((2, 32, n), bf), pltpu.VMEM((128, n), bf),
                         pltpu.VMEM((5,) + sums.shape, f32), pltpu.VMEM((5,) + sums.shape, f32),
-                        pltpu.VMEM((4, 2, 2, 2, 128, 512), bf), pltpu.VMEM((2, 2, tokens, tokens), bf),
+                        pltpu.VMEM((4, 2, 2, 2, 128, 512), bf), pltpu.VMEM((2, 2, 2, 2, 128, 512), bf), pltpu.VMEM((2, tokens, 512), bf),
+                        pltpu.VMEM((4, tokens, 512), bf), pltpu.VMEM((2, rows, width), bf), pltpu.VMEM((rows, width), f32), pltpu.VMEM((tokens, width), f32),
                         pltpu.VMEM((2, tokens, HD), bf), pltpu.VMEM((2, tokens, HD), f32), pltpu.VMEM((2, tokens, HD), f32),
                         pltpu.VMEM((2, tokens, HD), f32), pltpu.VMEM((4, tokens, 6 * HD), bf),
-                        pltpu.VMEM((rows, width), bf), pltpu.VMEM((rows, width), bf), pltpu.VMEM((rows, width), bf),
-                        pltpu.SemaphoreType.DMA((N_SCATTER,)), pltpu.SemaphoreType.DMA((N_SCATTER,)), pltpu.SemaphoreType.DMA((7,))],
+                        pltpu.VMEM((rows, width), bf), pltpu.VMEM((rows, width), bf), pltpu.VMEM((rows, width), bf), pltpu.VMEM((rows, width), bf), pltpu.VMEM((rows, width), bf),
+                        pltpu.SemaphoreType.DMA((N_SCATTER,)), pltpu.SemaphoreType.DMA((N_SCATTER,)), pltpu.SemaphoreType.DMA((19,))],
         compiler_params=pltpu.CompilerParams(collective_id=1, has_side_effects=True, vmem_limit_bytes=67043328),
         name="scatter",
-    )(second_low, hidden, norm_low, act_low, first_low, att, q, k, v, p_low, x, first_grad, full, lo, sums)
+    )(second_low, hidden, norm_low, slope, att, q, k, v, p_low.reshape(8, 2, 2, 128, tokens), x, first_sum, second_grad, gain, full, lo, sums)
 
 
 def swap_cores(value):
@@ -925,10 +972,10 @@
     small_full = small_full.reshape(4, 8, 16, 128)
     norm_all = small_full[0, :, :6].transpose(1, 0, 2).reshape(6, model_width).astype(f32)
     gain_rows, shift_rows = norm_all[:2], norm_all[2:]
-    full_up, full_down = (full[:, :, c0 : c0 + cn] for c0, cn in PIECES[2:])
+    full_down = full[:, :, PIECES[3][0] :]
     x_low = x_all.reshape(tokens, model_width)
     norm_low = norm_low.reshape(tokens, model_width)
-    first_norm, first_back = jax.vjp(norm_rows, first_sum, gain_rows[0], shift_rows[1])
+    first_norm = norm_rows(first_sum, gain_rows[0], shift_rows[1])
     down_part = dot32("tnc,tkc->nk", hidden, full_down)
     second_sum = first_norm + own_rows(down_part) + shift_rows[2]
     result, second_back = jax.vjp(norm_rows, second_sum, gain_rows[1], shift_rows[3])
@@ -936,23 +983,12 @@
     second_grad, gain_two, shift_three = second_back(upstream.astype(f32))
     shift_two = jnp.sum(second_grad, axis=0)
     second_low = both_rows(second_grad.astype(bf))
-    hidden_grad = dot32("nk,tkc->tnc", second_low, full_down)
-    act_grad = hidden_grad * gelu_slope.astype(f32)
-    up_bias_grad = jnp.sum(act_grad, axis=1)
-    act_low = act_grad.astype(bf)
-    back_part = dot32("tnc,tkc->nk", act_low, full_up)
-    norm_grad = second_grad + own_rows(back_part)
-    first_grad, gain_one, shift_one = first_back(norm_grad)
-    shift_zero = jnp.sum(first_grad, axis=0)
-    first_low = both_rows(first_grad.astype(bf))
-    norm_sums = jnp.stack([gain_one, gain_two, shift_zero, shift_one, shift_two, shift_three])
-    up_sums = jnp.stack([jnp.where(w.e == i, up_bias_grad, 0.0) for i in range(2)])
-    sums = jnp.concatenate(
-        [norm_sums.reshape(48, 128), jnp.zeros((16, 128), f32), up_sums.reshape(32, 128)]
-    )
+    blank = jnp.zeros_like(shift_two)
+    norm_sums = jnp.stack([blank, gain_two, blank, blank, shift_two, shift_three])
+    sums = jnp.concatenate([norm_sums.reshape(48, 128), jnp.zeros((48, 128), f32)])
     g_qkv, g_out, g_up, g_down, layer_out, input_out, sums = run_scatter(
-        second_low, hidden, norm_low, act_low, first_low, attended_low, queries, key_rows,
-        value_rows, p_low, x_low, first_grad, full_all, layer_mine, sums,
+        second_low, hidden, norm_low, gelu_slope, attended_low, queries, key_rows, value_rows,
+        p_low, x_low, first_sum, second_grad, gain_rows[:1], full_all, layer_mine, sums,
     )
     qv_mine = lax.dynamic_index_in_dim(sums[48:64].reshape(2, 4, 256), w.t, 1, keepdims=False)
     up_mine = lax.dynamic_index_in_dim(sums[64:].reshape(2, 4, 512), w.t, 1, keepdims=False)

time: 312 us -> 291 us (0.933)
  Pallas kernels: 265 us -> 257 us
  other arithmetic: 16.7 us -> 11.9 us
  matrix products: 9.42 us -> 4.63 us
  waiting for transfers between devices: 4.83 us -> 1.58 us
    pallas_call x1, Pallas kernels: 148 us -> 140 us  [run_scatter(): pl.pallas_call(scatter_kernel, out_shape=(sd((128, 768), f32), sd((128, 2...]
    dot_general x3 -> x1, matrix products: 9.42 us -> 4.63 us  [dot32(): return jnp.einsum(spec, left, right, preferred_element_type=jnp.float32)]
    ppermute x5 -> x3, waiting for transfers between devices: 4.83 us -> 1.58 us  [swap_cores(): lax.ppermute(value, 'fsdp', [(i, i ^ 1) for i in range(lax.axis_size('fsd...]
    unnamed x43 -> x27, local copies, waits for them, and re-layouts: 6.51 us -> 5.65 us
  transfers between devices with their start and end apart: 5 -> 3, of which waited for: 3 -> 2; matrix products, arithmetic and copies ran while one was open for 2% -> 2% of each run, Pallas kernels for 0% -> 0%
where the time goes in v1:
time: 291 us; the launch traced here: 290 us
  Pallas kernels  257 us (88%)
  local copies, waits for them, and re-layouts  13.5 us (5%)
  other arithmetic  11.9 us (4%)
  matrix products  4.63 us (2%)
    pallas_call x1, Pallas kernels, run_scatter(): pl.pallas_call(scatter_kernel, out_shape=(sd((128, 768), f32), sd((128, 2...  140 us
    pallas_call x1, Pallas kernels, run_gather(): pl.pallas_call(gather_kernel, out_shape=(sd((4, 2, 2, 2, 128, 1536), bf),...  117 us
  transfers between devices with their start and end apart: 3, of which 2 were waited for; matrix products, arithmetic and copies ran while one was open for 2% of the time, Pallas kernels for 0%

profile of v1, /device:TPU:0, one launch (start us, length us, event | category | flops | bytes accessed | tf_op | source)
XLA Modules:
  0.0 290.3 jit_solution(10748206533306079188)
XLA Ops:
  1.4 0.8 reshape.129
  2.3 0.7 maximum_bitcast_fusion
  3.0 1.4 maximum_maximum_fusion.small
  4.3 0.7 broadcast_select_fusion
  5.2 0.9 copy.31
  6.1 117.3 %gather.1 = (bf16[4,2,2,2,128,1536]{5,4,3,2,1,0:T(8,128)(2,1)}, bf16[4,2,2,2,16,128]{5,4,3,2,1,0:T(8,128)(2,1)}, bf16[2,256,1024]{2,1,0:T(8,128)(2,1)}, bf16[256...) custom-call(bf16[128,768]{1,0:T(8,128)(2,1)} %w_qkv.1, ...), custom_call_target="tpu_custom_call" | custom-call | tf_op jit(solution)/shard_map/gather/pallas_call | solution.py:596
  123.4 1.5 reduce_sum.78
  124.9 1.5 multiply_reduce_fusion.1
  126.4 4.6 %fusion.2 = f32[512,1024]{1,0:T(8,128)S(1)} fusion(bf16[4,512,512]{2,1,0:T(8,128)(2,1)S(1)} %copy-done.3, bf16[4,1024,1536]{2,1,0:T(8,128)(2,1)} %bitcast.59), kind=kOutput, calls=%fused_computation.2 | convolution fusion | flops 2147483648 | bytes 8388608 | tf_op jit(solution)/shard_map/tnc,tkc->nk/dot_general | solution.py:941
  131.2 0.8 slice.91
  134.1 1.4 fusion.8
  135.9 1.0 copy-done.1
  137.9 1.1 collective-permute-done.2
  138.9 1.0 pad_maximum_fusion.second_low
  140.0 139.7 %scatter.1 = (f32[128,768]{1,0:T(8,128)}, f32[128,256]{1,0:T(8,128)}, f32[128,1024]{1,0:T(8,128)}, f32[128,1024]{1,0:T(8,128)}, bf16[2,2,64,1024]{3,2,1,0:T(8,12...) custom-call(bf16[512,1024]{1,0:T(8,128)(2,1)} %pad_maximum_fusion.second_low, ...), custom_call_target="tpu_custom_call" | custom-call | tf_op jit(solution)/shard_map/scatter/pallas_call | solution.py:904
  279.7 0.8 slice.82
  280.5 0.7 slice.83
  281.2 0.7 slice_bitcast_fusion
  284.3 2.2 convert_element_type.33
  286.5 0.8 copy.41
  287.3 0.7 copy.42
  288.1 0.7 copy.43
  288.7 0.8 copy.44
  289.5 0.8 copy.45
  (59 shorter events, 7.0 us)
Async XLA Ops:
  0.6 3.7 %collective-permute-start = (s32[2,2,512]{2,1,0:T(2,128)}, s32[2,2,512]{2,1,0:T(2,128)S(1)}, u32[]{:S(2)}, u32[]{:S(2)}) collective-permute-start(s32[2,2,512]{2,1,0:T(2,128)} %param.13), channel_id=1, source_target_pairs={{0,8},{8,0},{16,24},{24,16},{1,9},{9,1},{17,25},{25,17},{2,10},{10... | collective-permute-start | bytes 24584 | tf_op jit(solution)/shard_map/ppermute | solution.py:928
  5.2 0.9 copy-start.9
  123.4 3.0 %copy-start.3 = (bf16[4,512,512]{2,1,0:T(8,128)(2,1)S(1)}, bf16[4,512,512]{2,1,0:T(8,128)(2,1)}, u32[]{:S(2)}) copy-start(bf16[4,512,512]{2,1,0:T(8,128)(2,1)} %get-tuple-element.33.hidden) | copy-start | bytes 6291460
  126.4 6.7 %copy-start = (f32[256,1024]{1,0:T(8,128)S(1)}, f32[256,1024]{1,0:T(8,128)}, u32[]{:S(2)}) copy-start(f32[256,1024]{1,0:T(8,128)} %get-tuple-element.32.first_sum) | copy-start | bytes 3145732
  131.1 2.5 copy-start.2
  131.1 2.0 collective-permute-start.1
  135.9 1.0 copy-start.1
  137.0 2.0 collective-permute-start.2
  279.7 6.9 %copy-start.6 = (bf16[2,2,64,1024]{3,2,1,0:T(8,128)(2,1)S(1)}, bf16[2,2,64,1024]{3,2,1,0:T(8,128)(2,1)}, u32[]{:S(2)}) copy-start(bf16[2,2,64,1024]{3,2,1,0:T(8,128)(2,1)} %get-tuple-element.80) | copy-start | bytes 1572868
  279.7 7.6 %copy-start.7 = (f32[128,768]{1,0:T(8,128)S(1)}, f32[128,768]{1,0:T(8,128)}, u32[]{:S(2)}) copy-start(f32[128,768]{1,0:T(8,128)} %get-tuple-element.82) | copy-start | bytes 1179652
  279.7 8.4 %copy-start.8 = (f32[128,256]{1,0:T(8,128)S(1)}, f32[128,256]{1,0:T(8,128)}, u32[]{:S(2)}) copy-start(f32[128,256]{1,0:T(8,128)} %get-tuple-element.84) | copy-start | bytes 393220
  279.7 9.0 %copy-start.5 = (f32[128,1024]{1,0:T(8,128)S(1)}, f32[128,1024]{1,0:T(8,128)}, u32[]{:S(2)}) copy-start(f32[128,1024]{1,0:T(8,128)} %get-tuple-element.85) | copy-start | bytes 1572868
  284.3 5.2 %copy-start.4 = (f32[128,1024]{1,0:T(8,128)S(1)}, f32[128,1024]{1,0:T(8,128)}, u32[]{:S(2)}) copy-start(f32[128,1024]{1,0:T(8,128)} %get-tuple-element.87) | copy-start | bytes 1572868
